TPU v7x, 32 devices: a whole 2x2x4 slice. The times are simulated.
32 devices in a mesh: dp: 4 (over z), ctx: 8 (over y, x, core).
Axes of the slice: x: 2, y: 2, z: 4, core: 2. Of those that a mesh axis runs over, the one named last changes fastest.
Arguments:
- tokens: bfloat16 [4, 1024, 8192], P('dp', 'ctx'), may hold values from -6 to 6
- w_down: bfloat16 [8192, 512], P(('dp', 'ctx')), may hold values from -0.0625 to 0.0625
- w_up: bfloat16 [512, 1024], replicated, may hold values from -0.25 to 0.25
- queries: bfloat16 [4, 1024, 4096], P('dp', 'ctx'), may hold values from -70 to 70, as said below
- block_order: int32 [4, 16], P('dp', 'ctx'), may hold values from 0 to 15, each once within a row
Outputs:
- attended: bfloat16 [4, 1024, 4096], P('dp', 'ctx')
Inputs may be any that keep to these rules, and one draw needn't show every extreme that they name: `queries`: query entries.
All inputs are finite; a program needn't handle non-finite values.
Results may differ from a plain program's by a relative error of at most 0.014.
The roundings to bfloat16 on the way count: a program that leaves them out, or rounds other values in their place, can miss the bound.
Values may be sent and summed in bfloat16 or wider, within the bound.
A program may use at most 64 MiB of HBM per device.

v0:
```python
import math
import jax
import jax.numpy as jnp
from jax import lax
from jax.sharding import PartitionSpec as P

QH = 32
KVH = 4
HD = 128


def per_device(tokens, w_down, w_up, queries, block_order):
    local_rows = tokens.shape[1]
    half_rows = local_rows // 2
    features = tokens[0]
    summed = jnp.dot(
        features,
        lax.all_gather(w_down, ("dp", "ctx"), axis=0, tiled=True),
        preferred_element_type=jnp.float32,
    )
    latent = summed.astype(jnp.bfloat16)
    order_whole = lax.all_gather(block_order, "ctx", axis=1, tiled=True)[0]
    block_count = order_whole.shape[0]
    local_ids = jnp.arange(local_rows, dtype=jnp.int32)
    query_pos = (
        jnp.where(local_ids < half_rows, block_order[0, 0], block_order[0, 1]) * half_rows
        + local_ids % half_rows
    )
    group = QH // KVH
    query_heads = queries[0].reshape(local_rows, KVH, group, HD).transpose(1, 2, 0, 3)
    score_scale = HD ** (-0.5)

    def update(carry, kv_block, key_pos):
        running_max, running_total, running_sum = carry
        width = kv_block.shape[0]
        key_block = kv_block[:, : KVH * HD].reshape(width, KVH, HD)
        value_block = kv_block[:, KVH * HD :].reshape(width, KVH, HD)
        scores = (
            jnp.einsum("kgsd,tkd->kgst", query_heads, key_block, preferred_element_type=jnp.float32)
            * score_scale
        )
        allowed = key_pos[None, :] <= query_pos[:, None]
        scores = jnp.where(allowed, scores, -1e30)
        new_max = jnp.maximum(running_max, jnp.max(scores, axis=-1))
        correction = jnp.exp(running_max - new_max)
        expo = jnp.where(allowed, jnp.exp(scores - new_max[..., None]), 0.0)
        new_total = running_total * correction + jnp.sum(expo, axis=-1)
        contrib = jnp.einsum(
            "kgst,tkd->kgsd",
            expo.astype(jnp.bfloat16),
            value_block,
            preferred_element_type=jnp.float32,
        )
        return (new_max, new_total, running_sum * correction[..., None] + contrib)

    start_state = (
        jnp.full((KVH, group, local_rows), -1e30, jnp.float32),
        jnp.zeros((KVH, group, local_rows), jnp.float32),
        jnp.zeros((KVH, group, local_rows, HD), jnp.float32),
    )
    kv_local = jnp.dot(latent, w_up, preferred_element_type=jnp.float32).astype(jnp.bfloat16)
    piece = lax.all_gather(kv_local, "ctx", axis=0, tiled=True)
    count = piece.shape[0]
    width = math.gcd(count, 256)
    blocks = piece.reshape(count // width, width, piece.shape[1])
    row_ids = jnp.arange(count, dtype=jnp.int32)
    onehot = (row_ids // half_rows)[:, None] == jnp.arange(block_count, dtype=jnp.int32)[None, :]
    block_ids = jnp.sum(jnp.where(onehot, order_whole[None, :], 0), axis=1)
    key_positions = (block_ids * half_rows + row_ids % half_rows).reshape(count // width, width)

    def step_block(state, inputs):
        block, key_pos = inputs
        state = update(state, block, key_pos)
        return (state, None)

    result, unused = lax.scan(step_block, start_state, (blocks, key_positions))
    unused_max, final_total, final_sum = result
    outputs = final_sum / final_total[..., None]
    return outputs.transpose(2, 0, 1, 3).reshape(1, local_rows, QH * HD).astype(jnp.bfloat16)


def solution(mesh):
    placed = (
        P("dp", "ctx", None),
        P(("dp", "ctx"), None),
        P(),
        P("dp", "ctx", None),
        P("dp", "ctx"),
    )
    return jax.shard_map(
        per_device, mesh=mesh, in_specs=placed, out_specs=P("dp", "ctx", None), check_vma=False
    )
```

profile of v0, /device:TPU:0, one launch (start us, length us, event | category | flops | bytes accessed | tf_op | source)
XLA Modules:
  0.0 171.8 jit_solution(13662498133776428902)
XLA Ops:
  7.3 83.1 %all-gather.3.cloned.1.call-done = bf16[8192,512]{1,0:T(8,128)(2,1)} async-done(((bf16[256,512]{1,0:T(8,128)(2,1)}), bf16[8192,512]{1,0:T(8,128)(2,1)}) %all-gather.3.cloned.1.call-update) | async-done | bytes 8388624 | tf_op jit(solution)/shard_map/all_gather | solution.py:18
  90.4 5.8 %convolution_convert_fusion = bf16[128,1024]{1,0:T(8,128)(2,1)} fusion(bf16[512,1024]{1,0:T(8,128)(2,1)} %param.9, bf16[8192,512]{1,0:T(8,128)(2,1)} %all-gather.3.cloned.1.call-done, bf16[1,128,8192]{2,1,0:T(8,128)(2,1)S(1)} %copy-done), kind=kOutput, calls=%fused_computation.31 | convolution fusion | flops 1208156160 | bytes 11796480 | tf_op jit(solution)/shard_map/dot_general | solution.py:61
  97.7 7.3 %all-reduce = s32[16]{0:T(128)S(1)} all-reduce(s32[16]{0:T(128)S(1)} %bitcast_dynamic-update-slice_fusion), channel_id=1, replica_groups=mesh['dp'=4,'ctx'=8] {'ctx'}, use_global_device_ids=true, to_apply=%add | all-reduce | flops 16 | bytes 128
  105.1 1.6 copy.18
  106.7 1.3 copy.20
  108.7 14.3 %all-gather.5.cloned.1.call-done = bf16[1024,1024]{1,0:T(8,128)(2,1)} async-done(((bf16[128,1024]{1,0:T(8,128)(2,1)}), bf16[1024,1024]{1,0:T(8,128)(2,1)}) %all-gather.5.cloned.1.call-update) | async-done | bytes 2097168 | tf_op jit(solution)/shard_map/all_gather | solution.py:62
  122.9 38.1 %while.15 = (s32[]{:T(128)}, f32[4,8,128]{2,1,0:T(8,128)S(1)}, f32[4,8,128]{2,1,0:T(8,128)S(1)}, f32[4,8,128,128]{3,2,1,0:T(8,128)}, s32[4,256]{1,0:T(4,128)S(1)...) while((s32[]{:T(128)}, f32[4,8,128]{2,1,0:T(8,128)S(1)}, ...), condition=%wide.region_4.5_spmd.clone, body=%wide.region_1.4_spmd.clone.sunk | while | flops 552129792 | bytes 38670536 | solution.py:76
  122.9 1.3 fusion.55
  124.3 1.1 constant_dynamic-slice_fusion.5
  125.7 2.2 %fusion.57 = (f32[4,8,128]{2,1,0:T(8,128)S(1)}, f32[4,256,8,128]{3,1,2,0:T(8,128)S(1)}) fusion(pred[128,256]{0,1:T(8,128)(4,1)S(1)} %broadcast_compare_fusion.2, bf16[256,4,128,1]{0,2,3,1:T(8,128)(2,1)S(1)} %bitcast.71, bf16[4,8,128,128]{3,2,1,0:T(8,128)(2,1)} %get-tuple-element.223), kind=kOutput, calls=%fused_computation.3.clone.1 | convolution fusion | flops 271577088 | bytes 5554176 | tf_op jit(solution)/shard_map/while/body/eval_jaxpr/kgsd,tkd->kgst/dot_general | solution.py:39
  127.9 1.1 fusion.58
  129.0 2.1 %fusion.60 = f32[4,8,128,128]{3,2,1,0:T(8,128)S(1)} fusion(f32[4,8,128,128]{3,2,1,0:T(8,128)S(1)} %copy-done.1, bf16[256,4,128,1]{0,2,3,1:T(8,128)(2,1)S(1)} %bitcast.72, f32[4,256,8,128]{3,1,2,0:T(8,128)S(1)} %get-tuple-element.191, f32[4,8,128]{2,1,0:T(8,128)S(1)} %select_maximum_fusion.2, pred[128,256]{0,1:T(8,128)(4,1)S(1)} %broadcast_compare_fusion.2, ...), kind=kOutput, calls=%fused_computation.8.clone.1 | convolution fusion | flops 275251200 | bytes 8716289 | tf_op jit(solution)/shard_map/while/body/eval_jaxpr/kgst,tkd->kgsd/dot_general | solution.py:48
  131.2 1.3 copy-done.2
  132.5 1.3 fusion.55
  133.9 1.1 constant_dynamic-slice_fusion.5
  135.2 2.2 %fusion.57 = (f32[4,8,128]{2,1,0:T(8,128)S(1)}, f32[4,256,8,128]{3,1,2,0:T(8,128)S(1)}) fusion(pred[128,256]{0,1:T(8,128)(4,1)S(1)} %broadcast_compare_fusion.2, bf16[256,4,128,1]{0,2,3,1:T(8,128)(2,1)S(1)} %bitcast.71, bf16[4,8,128,128]{3,2,1,0:T(8,128)(2,1)} %get-tuple-element.223), kind=kOutput, calls=%fused_computation.3.clone.1 | convolution fusion | flops 271577088 | bytes 5554176 | tf_op jit(solution)/shard_map/while/body/eval_jaxpr/kgsd,tkd->kgst/dot_general | solution.py:39
  137.5 1.1 fusion.58
  138.6 2.1 %fusion.60 = f32[4,8,128,128]{3,2,1,0:T(8,128)S(1)} fusion(f32[4,8,128,128]{3,2,1,0:T(8,128)S(1)} %copy-done.1, bf16[256,4,128,1]{0,2,3,1:T(8,128)(2,1)S(1)} %bitcast.72, f32[4,256,8,128]{3,1,2,0:T(8,128)S(1)} %get-tuple-element.191, f32[4,8,128]{2,1,0:T(8,128)S(1)} %select_maximum_fusion.2, pred[128,256]{0,1:T(8,128)(4,1)S(1)} %broadcast_compare_fusion.2, ...), kind=kOutput, calls=%fused_computation.8.clone.1 | convolution fusion | flops 275251200 | bytes 8716289 | tf_op jit(solution)/shard_map/while/body/eval_jaxpr/kgst,tkd->kgsd/dot_general | solution.py:48
  140.7 1.3 copy-done.2
  142.0 1.3 fusion.55
  143.4 1.1 constant_dynamic-slice_fusion.5
  144.8 2.2 %fusion.57 = (f32[4,8,128]{2,1,0:T(8,128)S(1)}, f32[4,256,8,128]{3,1,2,0:T(8,128)S(1)}) fusion(pred[128,256]{0,1:T(8,128)(4,1)S(1)} %broadcast_compare_fusion.2, bf16[256,4,128,1]{0,2,3,1:T(8,128)(2,1)S(1)} %bitcast.71, bf16[4,8,128,128]{3,2,1,0:T(8,128)(2,1)} %get-tuple-element.223), kind=kOutput, calls=%fused_computation.3.clone.1 | convolution fusion | flops 271577088 | bytes 5554176 | tf_op jit(solution)/shard_map/while/body/eval_jaxpr/kgsd,tkd->kgst/dot_general | solution.py:39
  147.0 1.1 fusion.58
  148.1 2.1 %fusion.60 = f32[4,8,128,128]{3,2,1,0:T(8,128)S(1)} fusion(f32[4,8,128,128]{3,2,1,0:T(8,128)S(1)} %copy-done.1, bf16[256,4,128,1]{0,2,3,1:T(8,128)(2,1)S(1)} %bitcast.72, f32[4,256,8,128]{3,1,2,0:T(8,128)S(1)} %get-tuple-element.191, f32[4,8,128]{2,1,0:T(8,128)S(1)} %select_maximum_fusion.2, pred[128,256]{0,1:T(8,128)(4,1)S(1)} %broadcast_compare_fusion.2, ...), kind=kOutput, calls=%fused_computation.8.clone.1 | convolution fusion | flops 275251200 | bytes 8716289 | tf_op jit(solution)/shard_map/while/body/eval_jaxpr/kgst,tkd->kgsd/dot_general | solution.py:48
  150.2 1.3 copy-done.2
  151.5 1.3 fusion.55
  152.9 1.1 constant_dynamic-slice_fusion.5
  154.3 2.2 %fusion.57 = (f32[4,8,128]{2,1,0:T(8,128)S(1)}, f32[4,256,8,128]{3,1,2,0:T(8,128)S(1)}) fusion(pred[128,256]{0,1:T(8,128)(4,1)S(1)} %broadcast_compare_fusion.2, bf16[256,4,128,1]{0,2,3,1:T(8,128)(2,1)S(1)} %bitcast.71, bf16[4,8,128,128]{3,2,1,0:T(8,128)(2,1)} %get-tuple-element.223), kind=kOutput, calls=%fused_computation.3.clone.1 | convolution fusion | flops 271577088 | bytes 5554176 | tf_op jit(solution)/shard_map/while/body/eval_jaxpr/kgsd,tkd->kgst/dot_general | solution.py:39
  157.6 2.1 %fusion.60 = f32[4,8,128,128]{3,2,1,0:T(8,128)S(1)} fusion(f32[4,8,128,128]{3,2,1,0:T(8,128)S(1)} %copy-done.1, bf16[256,4,128,1]{0,2,3,1:T(8,128)(2,1)S(1)} %bitcast.72, f32[4,256,8,128]{3,1,2,0:T(8,128)S(1)} %get-tuple-element.191, f32[4,8,128]{2,1,0:T(8,128)S(1)} %select_maximum_fusion.2, pred[128,256]{0,1:T(8,128)(4,1)S(1)} %broadcast_compare_fusion.2, ...), kind=kOutput, calls=%fused_computation.8.clone.1 | convolution fusion | flops 275251200 | bytes 8716289 | tf_op jit(solution)/shard_map/while/body/eval_jaxpr/kgst,tkd->kgsd/dot_general | solution.py:48
  159.7 1.3 copy-done.2
  161.0 1.9 %fusion.28 = bf16[128,4,8,128]{3,0,2,1:T(8,128)(2,1)S(1)} fusion(f32[4,8,128,128]{3,2,1,0:T(8,128)} %get-tuple-element.48, f32[4,8,128]{2,1,0:T(8,128)S(1)} %get-tuple-element.49), kind=kLoop, calls=%fused_computation.33 | loop fusion | flops 1048576 | bytes 3162112 | tf_op jit(solution)/shard_map/convert_element_type | solution.py:79
  163.7 1.3 convert_element_type.30
  (64 shorter events, 5.5 us)
Async XLA Ops:
  6.5 83.9 %copy-start = (bf16[1,128,8192]{2,1,0:T(8,128)(2,1)S(1)}, bf16[1,128,8192]{2,1,0:T(8,128)(2,1)}, u32[]{:S(2)}) copy-start(bf16[1,128,8192]{2,1,0:T(8,128)(2,1)} %param.7) | copy-start | bytes 6291460
  6.5 83.9 %all-gather.3.cloned.1.call-start = ((), (), s32[]{:S(2)}) async-start(), calls=%async_computation | async-start | bytes 8650752 | tf_op jit(solution)/shard_map/all_gather | solution.py:18
  7.3 89.0 %copy-start.4 = (u32[32]{0:T(128)S(1)}, u32[32]{0:T(128)}, u32[]{:S(2)}) copy-start(u32[32]{0:T(128)} %constant.71) | copy-start | bytes 388
  7.3 90.3 %copy-start.3 = (s32[1,2]{1,0:T(1,128)S(1)}, s32[1,2]{1,0:T(1,128)}, u32[]{:S(2)}) copy-start(s32[1,2]{1,0:T(1,128)} %param.11) | copy-start | bytes 28
  7.3 115.6 %all-gather.5.cloned.1.call-start = ((), (), s32[]{:S(2)}) async-start(), calls=%async_computation.1 | async-start | bytes 2359296 | tf_op jit(solution)/shard_map/all_gather | solution.py:62
  125.7 3.3 %copy-start.1 = (f32[4,8,128,128]{3,2,1,0:T(8,128)S(1)}, f32[4,8,128,128]{3,2,1,0:T(8,128)}, u32[]{:S(2)}) copy-start(f32[4,8,128,128]{3,2,1,0:T(8,128)} %get-tuple-element.209) | copy-start | bytes 6291460 | tf_op jit(solution)/shard_map/while
  131.2 1.3 copy-start.2
  135.2 3.3 %copy-start.1 = (f32[4,8,128,128]{3,2,1,0:T(8,128)S(1)}, f32[4,8,128,128]{3,2,1,0:T(8,128)}, u32[]{:S(2)}) copy-start(f32[4,8,128,128]{3,2,1,0:T(8,128)} %get-tuple-element.209) | copy-start | bytes 6291460 | tf_op jit(solution)/shard_map/while
  140.7 1.3 copy-start.2
  144.7 3.3 %copy-start.1 = (f32[4,8,128,128]{3,2,1,0:T(8,128)S(1)}, f32[4,8,128,128]{3,2,1,0:T(8,128)}, u32[]{:S(2)}) copy-start(f32[4,8,128,128]{3,2,1,0:T(8,128)} %get-tuple-element.209) | copy-start | bytes 6291460 | tf_op jit(solution)/shard_map/while
  150.2 1.3 copy-start.2
  154.3 3.3 %copy-start.1 = (f32[4,8,128,128]{3,2,1,0:T(8,128)S(1)}, f32[4,8,128,128]{3,2,1,0:T(8,128)}, u32[]{:S(2)}) copy-start(f32[4,8,128,128]{3,2,1,0:T(8,128)} %get-tuple-element.209) | copy-start | bytes 6291460 | tf_op jit(solution)/shard_map/while
  159.7 1.3 copy-start.2
Sparse Core Ops, SparseCore 0:
  10.2 80.1 all-gather.2
  96.4 26.4 all-gather.4
where the time goes:
time: 172 us
  waiting for transfers between devices  98.1 us (57%)
  matrix products  23.1 us (13%)
  local copies, waits for them, and re-layouts  16.7 us (10%)
  between operations  14.1 us (8%)
  other arithmetic  12 us (7%)
  blocking collectives  7.34 us (4%)
    all_gather x1, waiting for transfers between devices, per_device(): lax.all_gather(w_down, ('dp', 'ctx'), axis=0, tiled=True)  83.1 us
    all_gather x1, waiting for transfers between devices, per_device(): piece = lax.all_gather(kv_local, 'ctx', axis=0, tiled=True)  14.3 us
    dot_general x4, matrix products, update(): jnp.einsum('kgsd,tkd->kgst', query_heads, key_block, preferred_element_ty...  8.83 us
    dot_general x4, matrix products, update(): jnp.einsum('kgst,tkd->kgsd', expo.astype(jnp.bfloat16), value_block, pref...  8.43 us
    unnamed x1, blocking collectives  7.34 us
    dot_general x1, matrix products, per_device(): jnp.dot(latent, w_up, preferred_element_type=jnp.float32)  5.84 us
    dynamic_slice x12, local copies, waits for them, and re-layouts, per_device(): result, unused = lax.scan(step_block, start_state, (blocks, key_positions))  5.19 us
    while x20, local copies, waits for them, and re-layouts  5.18 us
  transfers between devices with their start and end apart: 2, of which 2 were waited for; matrix products, arithmetic and copies ran while one was open for 3% of the time, Pallas kernels for 0%

commit v1 on v0

--- a/solution.py
+++ b/solution.py
@@ -59,7 +59,14 @@
         jnp.zeros((KVH, group, local_rows, HD), jnp.float32),
     )
     kv_local = jnp.dot(latent, w_up, preferred_element_type=jnp.float32).astype(jnp.bfloat16)
-    piece = lax.all_gather(kv_local, "ctx", axis=0, tiled=True)
+    ways, here, step = (lax.axis_size("ctx"), lax.axis_index("ctx"), kv_local.shape[0])
+    line, have = (kv_local, 1)
+    while have < ways:
+        line = jnp.concatenate(
+            [line, lax.ppermute(line, "ctx", [(d, (d - have) % ways) for d in range(ways)])], axis=0
+        )
+        have = 2 * have
+    piece = jnp.roll(line, here * step, axis=0)
     count = piece.shape[0]
     width = math.gcd(count, 256)
     blocks = piece.reshape(count // width, width, piece.shape[1])

time: 172 us -> 228 us (1.33)
  blocking collectives: 7.34 us -> 23.8 us
  matrix products: 23.1 us -> 36.8 us
  other arithmetic: 12 us -> 23.2 us
  local copies, waits for them, and re-layouts: 16.7 us -> 24.8 us
  starting transfers between devices: 0.04 us -> 4.51 us
    unnamed x1, blocking collectives: 7.34 us -> 23.8 us
    ppermute x0 -> x3, waiting for transfers between devices: none -> 15.8 us  [per_device(): lax.ppermute(line, 'ctx', [(d, (d - have) % ways) for d in range(ways)])]
    all_gather x1 -> x0, waiting for transfers between devices: 14.3 us -> none  [per_device(): piece = lax.all_gather(kv_local, 'ctx', axis=0, tiled=True)]
    reduce_sum x4, other arithmetic: 4.29 us -> 13.6 us  [update(): new_total = running_total * correction + jnp.sum(expo, axis=-1)]
    unnamed x11 -> x17, local copies, waits for them, and re-layouts: 3.63 us -> 11.4 us
    dot_general x4, matrix products: 8.83 us -> 16 us  [update(): jnp.einsum('kgsd,tkd->kgst', query_heads, key_block, preferred_element_ty...]
    dot_general x4, matrix products: 8.43 us -> 15 us  [update(): jnp.einsum('kgst,tkd->kgsd', expo.astype(jnp.bfloat16), value_block, pref...]
    while x20 -> x12, local copies, waits for them, and re-layouts: 5.18 us -> 0.08 us
  transfers between devices with their start and end apart: 2 -> 4, of which waited for: 2 -> 3; matrix products, arithmetic and copies ran while one was open for 3% -> 3% of each run, Pallas kernels for 0% -> 0%
where the time goes in v1:
time: 228 us; the launch traced here: 227 us
  waiting for transfers between devices  99.7 us (44%)
  matrix products  36.8 us (16%)
  local copies, waits for them, and re-layouts  24.8 us (11%)
  blocking collectives  23.8 us (10%)
  other arithmetic  23.2 us (10%)
  between operations  14.1 us (6%)
  starting transfers between devices  4.51 us (2%)
    all_gather x1, waiting for transfers between devices, per_device(): lax.all_gather(w_down, ('dp', 'ctx'), axis=0, tiled=True)  83.1 us
    unnamed x1, blocking collectives  23.8 us
    dot_general x4, matrix products, update(): jnp.einsum('kgsd,tkd->kgst', query_heads, key_block, preferred_element_ty...  16 us
    ppermute x3, waiting for transfers between devices, per_device(): lax.ppermute(line, 'ctx', [(d, (d - have) % ways) for d in range(ways)])  15.8 us
    dot_general x4, matrix products, update(): jnp.einsum('kgst,tkd->kgsd', expo.astype(jnp.bfloat16), value_block, pref...  15 us
    reduce_sum x4, other arithmetic, update(): new_total = running_total * correction + jnp.sum(expo, axis=-1)  13.6 us
    unnamed x17, local copies, waits for them, and re-layouts  11.4 us
    dot_general x1, matrix products, per_device(): jnp.dot(latent, w_up, preferred_element_type=jnp.float32)  5.84 us
  transfers between devices with their start and end apart: 4, of which 3 were waited for; matrix products, arithmetic and copies ran while one was open for 3% of the time, Pallas kernels for 0%

profile of v1, /device:TPU:0, one launch (start us, length us, event | category | flops | bytes accessed | tf_op | source)
XLA Modules:
  0.0 227.1 jit_solution(10717955070420918946)
XLA Ops:
  7.3 83.1 %all-gather.2.cloned.1.call-done = bf16[8192,512]{1,0:T(8,128)(2,1)} async-done(((bf16[256,512]{1,0:T(8,128)(2,1)}), bf16[8192,512]{1,0:T(8,128)(2,1)}) %all-gather.2.cloned.1.call-update) | async-done | bytes 8388624 | tf_op jit(solution)/shard_map/all_gather | solution.py:18
  90.4 5.8 %constant_dynamic-update-slice_fusion.7 = (bf16[2048,1024]{1,0:T(8,128)(2,1)}, bf16[128,1024]{1,0:T(8,128)(2,1)S(1)}) fusion(bf16[512,1024]{1,0:T(8,128)(2,1)} %param.9, bf16[8192,512]{1,0:T(8,128)(2,1)} %all-gather.2.cloned.1.call-done, bf16[1,128,8192]{2,1,0:T(8,128)(2,1)S(1)} %copy-done), kind=kOutput, calls=%fused_computation.45 | convolution fusion | flops 1208156160 | bytes 12058624 | tf_op jit(solution)/shard_map/dot_general | solution.py:61
  96.3 1.3 collective-permute-start
  97.6 3.9 %collective-permute-done = bf16[128,1024]{1,0:T(8,128)(2,1)S(1)} collective-permute-done((bf16[128,1024]{1,0:T(8,128)(2,1)S(1)}, bf16[128,1024]{1,0:T(8,128)(2,1)S(1)}, u32[]{:S(2)}, u32[]{:S(2)}) %collective-permute-start) | collective-permute-done | bytes 262176 | tf_op jit(solution)/shard_map/ppermute | solution.py:66
  102.3 1.5 collective-permute-start.1
  105.0 11.9 %collective-permute-done.1 = bf16[256,1024]{1,0:T(8,128)(2,1)S(1)} collective-permute-done((bf16[256,1024]{1,0:T(8,128)(2,1)}, bf16[256,1024]{1,0:T(8,128)(2,1)S(1)}, u32[]{:S(2)}, u32[]{:S(2)}) %collective-permute-start.1) | collective-permute-done | bytes 524320 | tf_op jit(solution)/shard_map/ppermute | solution.py:66
  118.0 1.7 collective-permute-start.2
  119.8 23.8 %all-reduce = s32[16]{0:T(128)S(1)} all-reduce(s32[16]{0:T(128)S(1)} %bitcast_dynamic-update-slice_fusion), channel_id=1, replica_groups=mesh['dp'=4,'ctx'=8] {'ctx'}, use_global_device_ids=true, to_apply=%add | all-reduce | flops 16 | bytes 128
  143.7 2.3 %copy.24 = bf16[1,128,4096]{1,2,0:T(8,128)(2,1)} copy(bf16[1,128,4096]{2,1,0:T(8,128)(2,1)} %param.10) | data formatting | bytes 2097152 | tf_op args[3]
  146.0 2.3 %copy.26 = bf16[4,8,128,128]{3,2,1,0:T(8,128)(2,1)} copy(bf16[4,8,128,128]{2,3,1,0:T(8,128)(2,1)} %bitcast.76) | data formatting | bytes 2097152
  150.6 2.2 constant_dynamic-update-slice_fusion.4
  155.1 2.3 constant_dynamic-update-slice_fusion
  157.4 3.1 %constant_dynamic-slice_fusion.2 = bf16[1024,1024]{1,0:T(8,128)(2,1)} fusion(bf16[2048,1024]{1,0:T(8,128)(2,1)} %constant_dynamic-update-slice_fusion, s32[]{:T(128)S(6)} %select_n.56), kind=kLoop, calls=%fused_computation.60 | loop fusion | bytes 4194308 | tf_op jit(solution)/shard_map/jit(_roll_dynamic)/dynamic_slice | solution.py:69
  160.5 55.8 %while.15 = (s32[]{:T(128)}, f32[4,8,128]{2,1,0:T(8,128)S(1)}, f32[4,8,128]{2,1,0:T(8,128)S(1)}, f32[4,8,128,128]{3,2,1,0:T(8,128)}, s32[4,256]{1,0:T(4,128)S(1)...) while((s32[]{:T(128)}, f32[4,8,128]{2,1,0:T(8,128)S(1)}, ...), condition=%wide.region_4.5_spmd.clone, body=%wide.region_1.4_spmd.clone.sunk | while | flops 552129792 | bytes 38670500 | solution.py:83
  160.5 1.3 fusion.57
  163.2 4.0 %fusion.59 = (f32[4,8,128]{2,1,0:T(8,128)S(1)}, f32[4,256,8,128]{3,1,2,0:T(8,128)}) fusion(pred[128,256]{0,1:T(8,128)(4,1)S(1)} %broadcast_compare_fusion.2, bf16[256,4,128,1]{0,2,3,1:T(8,128)(2,1)S(1)} %bitcast.73, bf16[4,8,128,128]{3,2,1,0:T(8,128)(2,1)} %get-tuple-element.234), kind=kOutput, calls=%fused_computation.3.clone.1 | convolution fusion | flops 271577088 | bytes 5554176 | tf_op jit(solution)/shard_map/while/body/eval_jaxpr/kgsd,tkd->kgst/dot_general | solution.py:39
  167.2 3.4 %fusion.60 = f32[4,8,128]{2,1,0:T(8,128)S(1)} fusion(f32[4,256,8,128]{3,1,2,0:T(8,128)} %get-tuple-element.202, f32[4,8,128]{2,1,0:T(8,128)S(1)} %select_maximum_fusion.2, pred[128,256]{0,1:T(8,128)(4,1)S(1)} %broadcast_compare_fusion.2), kind=kLoop, calls=%fused_computation.5.clone.1 | loop fusion | flops 5238784 | bytes 4259840 | tf_op jit(solution)/shard_map/while/body/eval_jaxpr/reduce_sum | solution.py:47
  170.7 2.9 %fusion.62 = f32[4,8,128,128]{3,2,1,0:T(8,128)} fusion(f32[4,8,128,128]{3,2,1,0:T(8,128)} %get-tuple-element.220, bf16[256,4,128,1]{0,2,3,1:T(8,128)(2,1)S(1)} %bitcast.75, f32[4,256,8,128]{3,1,2,0:T(8,128)S(1)} %copy-done.1, f32[4,8,128]{2,1,0:T(8,128)S(1)} %select_maximum_fusion.2, pred[128,256]{0,1:T(8,128)(4,1)S(1)} %broadcast_compare_fusion.2, ...), kind=kOutput, calls=%fused_computation.8.clone.1 | convolution fusion | flops 275251200 | bytes 8716289 | tf_op jit(solution)/shard_map/while/body/eval_jaxpr/kgst,tkd->kgsd/dot_general | solution.py:48
  173.5 1.3 fusion.57
  176.3 4.0 %fusion.59 = (f32[4,8,128]{2,1,0:T(8,128)S(1)}, f32[4,256,8,128]{3,1,2,0:T(8,128)}) fusion(pred[128,256]{0,1:T(8,128)(4,1)S(1)} %broadcast_compare_fusion.2, bf16[256,4,128,1]{0,2,3,1:T(8,128)(2,1)S(1)} %bitcast.73, bf16[4,8,128,128]{3,2,1,0:T(8,128)(2,1)} %get-tuple-element.234), kind=kOutput, calls=%fused_computation.3.clone.1 | convolution fusion | flops 271577088 | bytes 5554176 | tf_op jit(solution)/shard_map/while/body/eval_jaxpr/kgsd,tkd->kgst/dot_general | solution.py:39
  180.3 3.4 %fusion.60 = f32[4,8,128]{2,1,0:T(8,128)S(1)} fusion(f32[4,256,8,128]{3,1,2,0:T(8,128)} %get-tuple-element.202, f32[4,8,128]{2,1,0:T(8,128)S(1)} %select_maximum_fusion.2, pred[128,256]{0,1:T(8,128)(4,1)S(1)} %broadcast_compare_fusion.2), kind=kLoop, calls=%fused_computation.5.clone.1 | loop fusion | flops 5238784 | bytes 4259840 | tf_op jit(solution)/shard_map/while/body/eval_jaxpr/reduce_sum | solution.py:47
  183.8 4.0 %fusion.62 = f32[4,8,128,128]{3,2,1,0:T(8,128)} fusion(f32[4,8,128,128]{3,2,1,0:T(8,128)} %get-tuple-element.220, bf16[256,4,128,1]{0,2,3,1:T(8,128)(2,1)S(1)} %bitcast.75, f32[4,256,8,128]{3,1,2,0:T(8,128)S(1)} %copy-done.1, f32[4,8,128]{2,1,0:T(8,128)S(1)} %select_maximum_fusion.2, pred[128,256]{0,1:T(8,128)(4,1)S(1)} %broadcast_compare_fusion.2, ...), kind=kOutput, calls=%fused_computation.8.clone.1 | convolution fusion | flops 275251200 | bytes 8716289 | tf_op jit(solution)/shard_map/while/body/eval_jaxpr/kgst,tkd->kgsd/dot_general | solution.py:48
  187.8 1.3 fusion.57
  190.6 4.0 %fusion.59 = (f32[4,8,128]{2,1,0:T(8,128)S(1)}, f32[4,256,8,128]{3,1,2,0:T(8,128)}) fusion(pred[128,256]{0,1:T(8,128)(4,1)S(1)} %broadcast_compare_fusion.2, bf16[256,4,128,1]{0,2,3,1:T(8,128)(2,1)S(1)} %bitcast.73, bf16[4,8,128,128]{3,2,1,0:T(8,128)(2,1)} %get-tuple-element.234), kind=kOutput, calls=%fused_computation.3.clone.1 | convolution fusion | flops 271577088 | bytes 5554176 | tf_op jit(solution)/shard_map/while/body/eval_jaxpr/kgsd,tkd->kgst/dot_general | solution.py:39
  194.6 3.4 %fusion.60 = f32[4,8,128]{2,1,0:T(8,128)S(1)} fusion(f32[4,256,8,128]{3,1,2,0:T(8,128)} %get-tuple-element.202, f32[4,8,128]{2,1,0:T(8,128)S(1)} %select_maximum_fusion.2, pred[128,256]{0,1:T(8,128)(4,1)S(1)} %broadcast_compare_fusion.2), kind=kLoop, calls=%fused_computation.5.clone.1 | loop fusion | flops 5238784 | bytes 4259840 | tf_op jit(solution)/shard_map/while/body/eval_jaxpr/reduce_sum | solution.py:47
  198.0 4.0 %fusion.62 = f32[4,8,128,128]{3,2,1,0:T(8,128)} fusion(f32[4,8,128,128]{3,2,1,0:T(8,128)} %get-tuple-element.220, bf16[256,4,128,1]{0,2,3,1:T(8,128)(2,1)S(1)} %bitcast.75, f32[4,256,8,128]{3,1,2,0:T(8,128)S(1)} %copy-done.1, f32[4,8,128]{2,1,0:T(8,128)S(1)} %select_maximum_fusion.2, pred[128,256]{0,1:T(8,128)(4,1)S(1)} %broadcast_compare_fusion.2, ...), kind=kOutput, calls=%fused_computation.8.clone.1 | convolution fusion | flops 275251200 | bytes 8716289 | tf_op jit(solution)/shard_map/while/body/eval_jaxpr/kgst,tkd->kgsd/dot_general | solution.py:48
  202.1 1.3 fusion.57
  204.8 4.0 %fusion.59 = (f32[4,8,128]{2,1,0:T(8,128)S(1)}, f32[4,256,8,128]{3,1,2,0:T(8,128)}) fusion(pred[128,256]{0,1:T(8,128)(4,1)S(1)} %broadcast_compare_fusion.2, bf16[256,4,128,1]{0,2,3,1:T(8,128)(2,1)S(1)} %bitcast.73, bf16[4,8,128,128]{3,2,1,0:T(8,128)(2,1)} %get-tuple-element.234), kind=kOutput, calls=%fused_computation.3.clone.1 | convolution fusion | flops 271577088 | bytes 5554176 | tf_op jit(solution)/shard_map/while/body/eval_jaxpr/kgsd,tkd->kgst/dot_general | solution.py:39
  208.8 3.4 %fusion.60 = f32[4,8,128]{2,1,0:T(8,128)S(1)} fusion(f32[4,256,8,128]{3,1,2,0:T(8,128)} %get-tuple-element.202, f32[4,8,128]{2,1,0:T(8,128)S(1)} %select_maximum_fusion.2, pred[128,256]{0,1:T(8,128)(4,1)S(1)} %broadcast_compare_fusion.2), kind=kLoop, calls=%fused_computation.5.clone.1 | loop fusion | flops 5238784 | bytes 4259840 | tf_op jit(solution)/shard_map/while/body/eval_jaxpr/reduce_sum | solution.py:47
  212.3 4.0 %fusion.62 = f32[4,8,128,128]{3,2,1,0:T(8,128)} fusion(f32[4,8,128,128]{3,2,1,0:T(8,128)} %get-tuple-element.220, bf16[256,4,128,1]{0,2,3,1:T(8,128)(2,1)S(1)} %bitcast.75, f32[4,256,8,128]{3,1,2,0:T(8,128)S(1)} %copy-done.1, f32[4,8,128]{2,1,0:T(8,128)S(1)} %select_maximum_fusion.2, pred[128,256]{0,1:T(8,128)(4,1)S(1)} %broadcast_compare_fusion.2, ...), kind=kOutput, calls=%fused_computation.8.clone.1 | convolution fusion | flops 275251200 | bytes 8716289 | tf_op jit(solution)/shard_map/while/body/eval_jaxpr/kgst,tkd->kgsd/dot_general | solution.py:48
  216.3 1.9 fusion.28
  219.0 1.3 convert_element_type.30
  (69 shorter events, 14.5 us)
Async XLA Ops:
  6.5 83.9 %copy-start = (bf16[1,128,8192]{2,1,0:T(8,128)(2,1)S(1)}, bf16[1,128,8192]{2,1,0:T(8,128)(2,1)}, u32[]{:S(2)}) copy-start(bf16[1,128,8192]{2,1,0:T(8,128)(2,1)} %param.7) | copy-start | bytes 6291460
  6.5 83.9 %all-gather.2.cloned.1.call-start = ((), (), s32[]{:S(2)}) async-start(), calls=%async_computation | async-start | bytes 8650752 | tf_op jit(solution)/shard_map/all_gather | solution.py:18
  7.3 96.5 %copy-start.3 = (u32[32]{0:T(128)S(1)}, u32[32]{0:T(128)}, u32[]{:S(2)}) copy-start(u32[32]{0:T(128)} %constant.98) | copy-start | bytes 388
  7.3 112.4 %copy-start.2 = (s32[1,2]{1,0:T(1,128)S(1)}, s32[1,2]{1,0:T(1,128)}, u32[]{:S(2)}) copy-start(s32[1,2]{1,0:T(1,128)} %param.11) | copy-start | bytes 28
  96.3 5.2 %collective-permute-start = (bf16[128,1024]{1,0:T(8,128)(2,1)S(1)}, bf16[128,1024]{1,0:T(8,128)(2,1)S(1)}, u32[]{:S(2)}, u32[]{:S(2)}) collective-permute-start(bf16[128,1024]{1,0:T(8,128)(2,1)S(1)} %get-tuple-element.138), channel_id=1, source_target_pairs={{0,7},{1,0},{2,1},{3,2},{4,3},{5,4},{6,5},{7,6},{8,15},{9,8},{10,9... | collective-permute-start | bytes 786440 | tf_op jit(solution)/shard_map/ppermute | solution.py:66
  102.3 14.6 %collective-permute-start.1 = (bf16[256,1024]{1,0:T(8,128)(2,1)}, bf16[256,1024]{1,0:T(8,128)(2,1)S(1)}, u32[]{:S(2)}, u32[]{:S(2)}) collective-permute-start(bf16[256,1024]{1,0:T(8,128)(2,1)} %pad_maximum_fusion.1), channel_id=1, source_target_pairs={{0,6},{1,7},{2,0},{3,1},{4,2},{5,3},{6,4},{7,5},{8,14},{9,15},{10,... | collective-permute-start | bytes 1572872 | tf_op jit(solution)/shard_map/ppermute | solution.py:66
  118.0 32.6 %collective-permute-start.2 = (bf16[512,1024]{1,0:T(8,128)(2,1)}, bf16[512,1024]{1,0:T(8,128)(2,1)}, u32[]{:S(2)}, u32[]{:S(2)}) collective-permute-start(bf16[512,1024]{1,0:T(8,128)(2,1)} %pad_maximum_fusion), channel_id=1, source_target_pairs={{0,4},{1,5},{2,6},{3,7},{4,0},{5,1},{6,2},{7,3},{8,12},{9,13},{10,... | collective-permute-start | bytes 3145736 | tf_op jit(solution)/shard_map/ppermute | solution.py:66
  167.2 3.4 %copy-start.1 = (f32[4,256,8,128]{3,1,2,0:T(8,128)S(1)}, f32[4,256,8,128]{3,1,2,0:T(8,128)}, u32[]{:S(2)}) copy-start(f32[4,256,8,128]{3,1,2,0:T(8,128)} %get-tuple-element.202) | copy-start | bytes 12582916 | tf_op jit(solution)/shard_map/while
  180.3 3.4 %copy-start.1 = (f32[4,256,8,128]{3,1,2,0:T(8,128)S(1)}, f32[4,256,8,128]{3,1,2,0:T(8,128)}, u32[]{:S(2)}) copy-start(f32[4,256,8,128]{3,1,2,0:T(8,128)} %get-tuple-element.202) | copy-start | bytes 12582916 | tf_op jit(solution)/shard_map/while
  194.6 3.4 %copy-start.1 = (f32[4,256,8,128]{3,1,2,0:T(8,128)S(1)}, f32[4,256,8,128]{3,1,2,0:T(8,128)}, u32[]{:S(2)}) copy-start(f32[4,256,8,128]{3,1,2,0:T(8,128)} %get-tuple-element.202) | copy-start | bytes 12582916 | tf_op jit(solution)/shard_map/while
  208.8 3.4 %copy-start.1 = (f32[4,256,8,128]{3,1,2,0:T(8,128)S(1)}, f32[4,256,8,128]{3,1,2,0:T(8,128)}, u32[]{:S(2)}) copy-start(f32[4,256,8,128]{3,1,2,0:T(8,128)} %get-tuple-element.202) | copy-start | bytes 12582916 | tf_op jit(solution)/shard_map/while
Sparse Core Ops, SparseCore 0:
  10.2 80.1 all-gather.1
